TPU v7x, 512 devices: a whole 4x8x8 slice. The times are simulated.
512 devices in a mesh: dp: 16 (over y, core), lat: 32 (over z, x).
Axes of the slice: x: 4, y: 8, z: 8, core: 2. Of those that a mesh axis runs over, the one named last changes fastest.
Arguments:
- fields: bfloat16 [16, 96, 180, 768], P('dp', 'lat'), may hold values from -6 to 6
- cotangent: bfloat16 [16, 96, 180, 768], P('dp', 'lat'), may hold values from -6 to 6
- w_first: bfloat16 [2, 8, 96, 96], replicated, may hold values from -0.4375 to 0.4375
- b_first: float32 [2, 768], replicated, may hold values from -3 to 3
- w_second: bfloat16 [2, 8, 96, 96], replicated, may hold values from -0.4375 to 0.4375
- b_second: float32 [2, 768], replicated, may hold values from -3 to 3
Outputs:
- output: bfloat16 [16, 96, 180, 768], P('dp', 'lat')
- grad_fields: bfloat16 [16, 96, 180, 768], P('dp', 'lat')
- grad_w_first: float32 [2, 8, 96, 96], replicated
- grad_b_first: float32 [2, 768], replicated
- grad_w_second: float32 [2, 8, 96, 96], replicated
- grad_b_second: float32 [2, 768], replicated
All inputs are finite; a program needn't handle non-finite values.
Results may differ from a plain program's by a relative error of at most 0.015.
Values may be sent and summed in bfloat16 or wider, within the bound.
No kernel may reach another device: no remote copies, remote signals or barrier semaphores. Data moves between devices by JAX's collectives and lax.ppermute only.
A program may use at most 64 MiB of HBM per device.

v0:
```python
from functools import partial
import math
import jax
import jax.numpy as jnp
from jax import lax
from jax.sharding import PartitionSpec as P

C = 768
NB = 8
BS = 96
H = 96
W = 180
KX = 64
EPSILON = 1e-06


def layer_norm(values):
    centered = values - jnp.mean(values, axis=-1, keepdims=True)
    spread = jnp.mean(centered * centered, axis=-1, keepdims=True)
    return centered / jnp.sqrt(spread + EPSILON)


def angles(count_left, count_right, period):
    left_index = jnp.arange(count_left, dtype=jnp.int32)[:, None]
    right_index = jnp.arange(count_right, dtype=jnp.int32)[None, :]
    return 2.0 * math.pi / period * (left_index * right_index % period).astype(jnp.float32)


def longitude_tables(mode_count):
    angle_grid = angles(W, mode_count, W)
    mode_index = jnp.arange(mode_count, dtype=jnp.int32)[None, :]
    live_modes = jnp.where(mode_index <= W // 2, 1.0, 0.0).astype(jnp.float32) / math.sqrt(W)
    weight = jnp.where(mode_index == 0, 1.0, 2.0).astype(jnp.float32) * live_modes
    forward = jnp.stack(
        [jnp.cos(angle_grid) * live_modes, -jnp.sin(angle_grid) * live_modes], axis=2
    )
    inverse = jnp.stack([jnp.cos(angle_grid) * weight, -jnp.sin(angle_grid) * weight], axis=2)
    return (forward.astype(jnp.bfloat16), inverse.astype(jnp.bfloat16))


def latitude_table():
    angle_grid = angles(H, H, H)
    cosine = jnp.cos(angle_grid) / math.sqrt(H)
    sine_part = jnp.sin(angle_grid) / math.sqrt(H)
    real_row = jnp.stack([cosine, sine_part], axis=2)
    imag_row = jnp.stack([-sine_part, cosine], axis=2)
    return jnp.stack([real_row, imag_row], axis=1).astype(jnp.bfloat16)


def real_form(weight):
    real_part = weight[0]
    imag_part = weight[1]
    upper_rows = jnp.stack([real_part, imag_part], axis=2)
    lower_rows = jnp.stack([-imag_part, real_part], axis=2)
    return jnp.stack([upper_rows, lower_rows], axis=1)


def fold_grads(gathered):
    real_grad = gathered[:, 0, :, 0, :] + gathered[:, 1, :, 1, :]
    imag_grad = gathered[:, 0, :, 1, :] - gathered[:, 1, :, 0, :]
    return jnp.stack([real_grad, imag_grad], axis=0)


def product(pattern, left_side, right_side):
    return jnp.einsum(pattern, left_side, right_side, preferred_element_type=jnp.float32)


def spectral_forward(spectra_modes, first_form, bias_one, second_form, bias_two):
    leading = spectra_modes.shape[:3]
    blocked = spectra_modes.reshape(leading + (2, NB, BS))
    pre_one = (
        product("bmkqni,nqipo->bmkpno", blocked, first_form).reshape(leading + (2, C)) + bias_one
    )
    hidden = jax.nn.gelu(pre_one, approximate=False).astype(jnp.bfloat16)
    pre_two = (
        product("bmkqni,nqipo->bmkpno", hidden.reshape(leading + (2, NB, BS)), second_form).reshape(
            leading + (2, C)
        )
        + bias_two
    )
    return (pre_one, hidden, pre_two)


def spectral_backward(spectra_modes, pre_one, hidden, first_form, second_form, back_filtered):
    leading = spectra_modes.shape[:3]
    back_blocked = back_filtered.reshape(leading + (2, NB, BS))
    grad_second = product(
        "bmkqni,bmkpno->nqipo", hidden.reshape(leading + (2, NB, BS)), back_blocked
    )
    bias_two_grad = jnp.sum(back_filtered.astype(jnp.float32), axis=(0, 1, 2))
    back_hidden = product("bmkpno,nqipo->bmkqni", back_blocked, second_form).reshape(
        leading + (2, C)
    )
    unused, gelu_back = jax.vjp(partial(jax.nn.gelu, approximate=False), pre_one)
    back_pre = gelu_back(back_hidden)[0].astype(jnp.bfloat16)
    pre_blocked = back_pre.reshape(leading + (2, NB, BS))
    grad_first = product(
        "bmkqni,bmkpno->nqipo", spectra_modes.reshape(leading + (2, NB, BS)), pre_blocked
    )
    bias_one_grad = jnp.sum(back_pre.astype(jnp.float32), axis=(0, 1, 2))
    back_modes = (
        product("bmkpno,nqipo->bmkqni", pre_blocked, first_form)
        .reshape(leading + (2, C))
        .astype(jnp.bfloat16)
    )
    return (
        fold_grads(grad_first),
        bias_one_grad,
        fold_grads(grad_second),
        bias_two_grad,
        back_modes,
    )


def on_device(fields, cotangent, w_first, b_first, w_second, b_second):
    band_count = lax.axis_size("lat")
    mode_count = (W // 2 + band_count) // band_count * band_count
    local_modes = mode_count // band_count
    mode_index = lax.axis_index("lat") * local_modes + jnp.arange(local_modes, dtype=jnp.int32)
    mode_mask = (
        jnp.where(mode_index < KX, 1.0, 0.0).astype(jnp.float32).reshape(1, 1, local_modes, 1, 1)
    )
    forward_lon, inverse_lon = longitude_tables(mode_count)
    latitude = latitude_table()
    first_form = real_form(w_first)
    second_form = real_form(w_second)
    values = fields.astype(jnp.float32)
    normed, norm_back = jax.vjp(layer_norm, values)
    spectra = product("bhwc,wkp->bhkpc", normed.astype(jnp.bfloat16), forward_lon).astype(
        jnp.bfloat16
    )
    column_spectra = lax.all_to_all(spectra, "lat", split_axis=2, concat_axis=1, tiled=True)
    spectra_modes = product("mqhp,bhkpc->bmkqc", latitude, column_spectra).astype(jnp.bfloat16)
    pre_one, hidden, pre_two = spectral_forward(
        spectra_modes, first_form, b_first, second_form, b_second
    )
    filtered = (pre_two * mode_mask).astype(jnp.bfloat16)
    column_rows = product("mphq,bmkpc->bhkqc", latitude, filtered).astype(jnp.bfloat16)
    row_spectra = lax.all_to_all(column_rows, "lat", split_axis=1, concat_axis=2, tiled=True)
    mixed = product("bhkpc,wkp->bhwc", row_spectra, inverse_lon)
    result = (values + normed + mixed).astype(jnp.bfloat16)
    upstream = cotangent.astype(jnp.float32)
    back_rows = product("bhwc,wkp->bhkpc", cotangent, inverse_lon).astype(jnp.bfloat16)
    back_columns = lax.all_to_all(back_rows, "lat", split_axis=2, concat_axis=1, tiled=True)
    back_filtered = (product("mphq,bhkqc->bmkpc", latitude, back_columns) * mode_mask).astype(
        jnp.bfloat16
    )
    grad_one, bias_one, grad_two, bias_two, back_modes = spectral_backward(
        spectra_modes, pre_one, hidden, first_form, second_form, back_filtered
    )
    back_column_rows = product("mqhp,bmkqc->bhkpc", latitude, back_modes).astype(jnp.bfloat16)
    back_spectra = lax.all_to_all(back_column_rows, "lat", split_axis=1, concat_axis=2, tiled=True)
    back_normed = upstream + product("bhkpc,wkp->bhwc", back_spectra, forward_lon)
    back_fields = (upstream + norm_back(back_normed)[0]).astype(jnp.bfloat16)
    grad_scale = 1.0 / (fields.shape[0] * lax.axis_size("dp") * H)
    members = (grad_one, bias_one, grad_two, bias_two)
    packed = jnp.concatenate([member.reshape(-1) for member in members]) * grad_scale
    all_grads = lax.psum(packed, ("dp", "lat"))
    results = []
    offset = 0
    for member in members:
        length = member.size
        results.append(all_grads[offset : offset + length].reshape(member.shape))
        offset = offset + length
    return (result, back_fields, results[0], results[1], results[2], results[3])


def solution(mesh):
    placed = (P("dp", "lat", None, None), P("dp", "lat", None, None), P(), P(), P(), P())
    return jax.shard_map(
        on_device,
        mesh=mesh,
        in_specs=placed,
        out_specs=(P("dp", "lat", None, None), P("dp", "lat", None, None), P(), P(), P(), P()),
        check_vma=False,
    )
```

profile of v0, /device:TPU:1, one launch (start us, length us, event | category | flops | bytes accessed | tf_op | source)
XLA Modules:
  0.0 435.8 jit_solution(13082725453070378187)
XLA Ops:
  8.5 1.6 fusion.34
  12.4 1.7 fusion.40
  14.1 1.8 copy.151
  16.0 13.7 %all-to-all-start = ((bf16[1,3,96,2,768]{4,3,1,0,2:T(2,128)(2,1)}), bf16[1,3,96,2,768]{4,3,1,0,2:T(2,128)(2,1)S(1)}, u32[]{:S(2)}, u32[]{:S(2)}) async-start(bf16[1,3,96,2,768]{4,3,1,0,2:T(2,128)(2,1)} %copy.151), calls=%async_computation | async-start | bytes 1769472 | tf_op jit(solution)/shard_map/all_to_all | solution.py:132
  31.2 1.8 copy.163
  33.1 19.5 %all-to-all-done = bf16[1,3,96,2,768]{4,3,1,0,2:T(2,128)(2,1)S(1)} async-done(((bf16[1,3,96,2,768]{4,3,1,0,2:T(2,128)(2,1)}), bf16[1,3,96,2,768]{4,3,1,0,2:T(2,128)(2,1)S(1)}, u32[]{:S(2)}, u32[]{:S(2)}) %all-to-all-start) | async-done | bytes 884768 | tf_op jit(solution)/shard_map/all_to_all | solution.py:132
  52.6 6.1 %all-to-all-start.2 = ((bf16[1,3,96,2,768]{4,3,1,0,2:T(2,128)(2,1)}), bf16[1,3,96,2,768]{4,3,1,0,2:T(2,128)(2,1)S(1)}, u32[]{:S(2)}, u32[]{:S(2)}) async-start(bf16[1,3,96,2,768]{4,3,1,0,2:T(2,128)(2,1)} %copy.163), calls=%async_computation.2 | async-start | bytes 1769472 | tf_op jit(solution)/shard_map/all_to_all | solution.py:144
  67.7 2.2 reshape.652
  69.9 10.8 %all-to-all-done.2 = bf16[1,3,96,2,768]{4,3,1,0,2:T(2,128)(2,1)S(1)} async-done(((bf16[1,3,96,2,768]{4,3,1,0,2:T(2,128)(2,1)}), bf16[1,3,96,2,768]{4,3,1,0,2:T(2,128)(2,1)S(1)}, u32[]{:S(2)}, u32[]{:S(2)}) %all-to-all-start.2) | async-done | bytes 884768 | tf_op jit(solution)/shard_map/all_to_all | solution.py:144
  83.4 2.4 reshape.658
  85.8 6.8 %fusion.5 = (f32[96,3,2,8,96]{4,0,1,2,3:T(8,128)S(1)}, f32[8,2,96,96,3,1]{2,3,5,4,1,0:T(8,128)S(1)}) fusion(f32[2,8,96]{2,0,1:T(2,128)S(1)} %copy-done.23, bf16[96,3,2,8,96,1]{4,3,0,2,1,5:T(8,128)(2,1)} %bitcast.367, bf16[8,1,96,2,96]{4,2,1,3,0:T(8,128)(2,1)S(1)} %copy-done.13, bf16[8,1,96,2,96]{4,2,1,3,0:T(8,128)(2,1)S(1)} %copy-done.11), kind=kOutput, calls=%fused_computation.11 | convolution fusion | flops 198918144 | bytes 5019648 | tf_op jit(solution)/shard_map/bmkqni,nqipo->bmkpno/dot_general | solution.py:65
  94.4 8.0 %convert_reduce_fusion.1 = (f32[2,8,96]{2,0,1:T(2,128)}, bf16[1,96,3,2,8,96]{5,1,2,3,4,0:T(8,128)(2,1)}, f32[1,96,3,2,8,96]{5,1,2,3,4,0:T(8,128)}, f32[8,2,96,96,3,1]{2,3,5,4,1,0:T(8,128)S(1)}) fusion(f32[2,8,96]{2,0,1:T(2,128)S(1)} %copy-done.23, f32[8,2,96,96,3,1]{2,3,5,4,1,0:T(8,128)S(1)} %get-tuple-element.35, ...), kind=kOutput, calls=%fused_computation.34 | convolution fusion | flops 203340288 | bytes 7680000 | tf_op jit(solution)/shard_map/bmkpno,nqipo->bmkqni/dot_general | solution.py:65
  102.5 1.7 convolution_bitcast_fusion.2
  107.8 3.2 convolution_bitcast_fusion
  111.0 2.0 copy.158
  113.0 2.1 reshape.654
  115.6 1.8 copy.160
  118.1 6.6 %all-to-all-start.1 = ((bf16[1,96,3,2,768]{4,3,2,0,1:T(2,128)(2,1)}), bf16[1,96,3,2,768]{4,3,2,0,1:T(2,128)(2,1)S(1)}, u32[]{:S(2)}, u32[]{:S(2)}) async-start(bf16[1,96,3,2,768]{4,3,2,0,1:T(2,128)(2,1)} %copy.160), calls=%async_computation.1 | async-start | bytes 1769472 | tf_op jit(solution)/shard_map/all_to_all | solution.py:139
  127.2 2.3 maximum_multiply_fusion
  129.6 2.9 fusion.39
  132.5 1.8 copy.171
  134.3 1.9 reshape.694
  136.2 1.6 fusion.45
  137.8 1.8 copy.173
  139.7 6.8 %all-to-all-done.1 = bf16[1,96,3,2,768]{4,3,2,0,1:T(2,128)(2,1)S(1)} async-done(((bf16[1,96,3,2,768]{4,3,2,0,1:T(2,128)(2,1)}), bf16[1,96,3,2,768]{4,3,2,0,1:T(2,128)(2,1)S(1)}, u32[]{:S(2)}, u32[]{:S(2)}) %all-to-all-start.1) | async-done | bytes 884768 | tf_op jit(solution)/shard_map/all_to_all | solution.py:139
  146.5 6.9 %all-to-all-start.3 = ((bf16[1,96,3,2,768]{4,3,2,0,1:T(2,128)(2,1)}), bf16[1,96,3,2,768]{4,3,2,0,1:T(2,128)(2,1)}, u32[]{:S(2)}, u32[]{:S(2)}) async-start(bf16[1,96,3,2,768]{4,3,2,0,1:T(2,128)(2,1)} %copy.173), calls=%async_computation.3 | async-start | bytes 1769472 | tf_op jit(solution)/shard_map/all_to_all | solution.py:152
  153.4 261.3 %all-reduce.2.cloned.1.call-done = f32[297984]{0:T(1024)} async-done(((f32[297984]{0:T(1024)}), f32[297984]{0:T(1024)}) %all-reduce.2.cloned.1.call-update) | async-done | bytes 1191952 | tf_op jit(solution)/shard_map/psum | solution.py:158
  414.7 2.1 fusion.121
  418.8 2.2 reshape.668
  422.8 1.4 fusion.37
  424.2 1.8 copy.174
  427.4 1.6 fusion.33
  (119 shorter events, 30.7 us)
Async XLA Ops:
  14.1 16.7 %copy-start.2 = (bf16[1,3,180,768]{3,2,1,0:T(8,128)(2,1)S(1)}, bf16[1,3,180,768]{3,2,1,0:T(8,128)(2,1)}, u32[]{:S(2)}) copy-start(bf16[1,3,180,768]{3,2,1,0:T(8,128)(2,1)} %param.7) | copy-start | bytes 2488324
  16.0 36.7 %all-to-all-start = ((bf16[1,3,96,2,768]{4,3,1,0,2:T(2,128)(2,1)}), bf16[1,3,96,2,768]{4,3,1,0,2:T(2,128)(2,1)S(1)}, u32[]{:S(2)}, u32[]{:S(2)}) async-start(bf16[1,3,96,2,768]{4,3,1,0,2:T(2,128)(2,1)} %copy.151), calls=%async_computation | async-start | bytes 1769472 | tf_op jit(solution)/shard_map/all_to_all | solution.py:132
  31.2 28.6 %copy-start.30 = (f32[2,768]{1,0:T(2,128)S(1)}, f32[2,768]{1,0:T(2,128)}, u32[]{:S(2)}) copy-start(f32[2,768]{1,0:T(2,128)} %param.9) | copy-start | bytes 18436
  52.6 28.1 %all-to-all-start.2 = ((bf16[1,3,96,2,768]{4,3,1,0,2:T(2,128)(2,1)}), bf16[1,3,96,2,768]{4,3,1,0,2:T(2,128)(2,1)S(1)}, u32[]{:S(2)}, u32[]{:S(2)}) async-start(bf16[1,3,96,2,768]{4,3,1,0,2:T(2,128)(2,1)} %copy.163), calls=%async_computation.2 | async-start | bytes 1769472 | tf_op jit(solution)/shard_map/all_to_all | solution.py:144
  61.8 53.3 %copy-start.9 = (bf16[96,1,96,2]{2,0,3,1:T(8,128)(2,1)}, bf16[96,1,96,2]{2,0,3,1:T(8,128)(2,1)S(1)}, u32[]{:S(2)}) copy-start(bf16[96,1,96,2]{2,0,3,1:T(8,128)(2,1)S(1)} %get-tuple-element.22) | copy-start | bytes 110596
  62.8 31.5 %copy-start.4 = (bf16[8,1,96,2,96]{2,4,1,3,0:T(8,128)(2,1)}, bf16[8,1,96,2,96]{2,4,1,3,0:T(8,128)(2,1)S(1)}, u32[]{:S(2)}) copy-start(bf16[8,1,96,2,96]{2,4,1,3,0:T(8,128)(2,1)S(1)} %get-tuple-element.19) | copy-start | bytes 884740
  67.6 14.3 %copy-start.32 = (f32[3]{0:T(128)S(1)}, f32[3]{0:T(128)}, u32[]{:S(2)}) copy-start(f32[3]{0:T(128)} %compare_select_fusion) | copy-start | bytes 40
  82.0 3.8 copy-start.11
  82.0 3.8 copy-start.13
  82.0 3.8 copy-start.23
  92.6 9.9 %copy-start.1 = (f32[8,2,96,96,3,1]{2,3,5,4,1,0:T(8,128)}, f32[8,2,96,96,3,1]{2,3,5,4,1,0:T(8,128)S(1)}, u32[]{:S(2)}) copy-start(f32[8,2,96,96,3,1]{2,3,5,4,1,0:T(8,128)S(1)} %get-tuple-element.35) | copy-start | bytes 5308420
  93.4 1.0 copy-start.5
  94.4 8.0 %copy-start.8 = (bf16[96,3,2,8,96]{4,3,0,2,1:T(8,128)(2,1)S(1)}, bf16[96,3,2,8,96]{4,3,0,2,1:T(8,128)(2,1)}, u32[]{:S(2)}) copy-start(bf16[96,3,2,8,96]{4,3,0,2,1:T(8,128)(2,1)} %reshape.652) | copy-start | bytes 2654212
  104.2 2.2 copy-start.7
  113.0 2.1 copy-start.31
  115.1 2.3 copy-start.29
  115.6 9.2 %copy-start.6 = (f32[1,8,96,96]{3,2,1,0:T(8,128)S(1)}, f32[1,8,96,96]{3,2,1,0:T(8,128)}, u32[]{:S(2)}) copy-start(f32[1,8,96,96]{3,2,1,0:T(8,128)} %fusion.84) | copy-start | bytes 884740
  118.1 9.1 %copy-start.3 = (f32[147456]{0:T(1024)S(1)}, f32[147456]{0:T(1024)}, u32[]{:S(2)}) copy-start(f32[147456]{0:T(1024)} %reshape.665) | copy-start | bytes 1769476
  118.1 28.3 %all-to-all-start.1 = ((bf16[1,96,3,2,768]{4,3,2,0,1:T(2,128)(2,1)}), bf16[1,96,3,2,768]{4,3,2,0,1:T(2,128)(2,1)S(1)}, u32[]{:S(2)}, u32[]{:S(2)}) async-start(bf16[1,96,3,2,768]{4,3,2,0,1:T(2,128)(2,1)} %copy.160), calls=%async_computation.1 | async-start | bytes 1769472 | tf_op jit(solution)/shard_map/all_to_all | solution.py:139
  124.8 289.9 %all-reduce.2.cloned.1.call-start = ((), (), s32[]{:S(2)}) async-start(), calls=%async_computation.4 | async-start | bytes 2383872 | tf_op jit(solution)/shard_map/psum | solution.py:158
  125.9 3.6 copy-start.12
  127.2 2.4 copy-start.14
  132.5 3.7 copy-start.10
  146.5 277.8 %all-to-all-start.3 = ((bf16[1,96,3,2,768]{4,3,2,0,1:T(2,128)(2,1)}), bf16[1,96,3,2,768]{4,3,2,0,1:T(2,128)(2,1)}, u32[]{:S(2)}, u32[]{:S(2)}) async-start(bf16[1,96,3,2,768]{4,3,2,0,1:T(2,128)(2,1)} %copy.173), calls=%async_computation.3 | async-start | bytes 1769472 | tf_op jit(solution)/shard_map/all_to_all | solution.py:152
  416.8 5.9 %copy-start = (bf16[1,3,180,768]{3,2,1,0:T(8,128)(2,1)S(1)}, bf16[1,3,180,768]{3,2,1,0:T(8,128)(2,1)}, u32[]{:S(2)}) copy-start(bf16[1,3,180,768]{3,2,1,0:T(8,128)(2,1)} %param.6) | copy-start | bytes 2488324
  416.8 5.9 %copy-start.20 = (bf16[180,96,1]{1,0,2:T(8,128)(2,1)S(1)}, bf16[180,96,1]{1,0,2:T(8,128)(2,1)}, u32[]{:S(2)}) copy-start(bf16[180,96,1]{1,0,2:T(8,128)(2,1)} %copy-done.19) | copy-start | bytes 103684
  416.8 5.9 %copy-start.22 = (bf16[180,96,1]{1,0,2:T(8,128)(2,1)S(1)}, bf16[180,96,1]{1,0,2:T(8,128)(2,1)}, u32[]{:S(2)}) copy-start(bf16[180,96,1]{1,0,2:T(8,128)(2,1)} %copy-done.21) | copy-start | bytes 103684
  416.8 5.9 %copy-start.25 = (f32[3,180]{1,0:T(4,128)S(1)}, f32[3,180]{1,0:T(4,128)}, u32[]{:S(2)}) copy-start(f32[3,180]{1,0:T(4,128)} %copy-done.24) | copy-start | bytes 6484
  422.8 3.2 copy-start.16
  422.8 3.2 copy-start.18
  422.8 3.2 copy-start.28
  426.0 0.8 copy-start.27
  (6 other events, 3.7 us)
Sparse Core Ops, SparseCore 0:
  130.7 283.9 all-reduce.1
where the time goes:
time: 437 us; the launch traced here: 436 us
  waiting for transfers between devices  298 us (68%)
  local copies, waits for them, and re-layouts  41 us (9%)
  starting transfers between devices  33.5 us (8%)
  matrix products  31.7 us (7%)
  other arithmetic  16.5 us (4%)
  between operations  14.6 us (3%)
    psum x1, waiting for transfers between devices, on_device(): all_grads = lax.psum(packed, ('dp', 'lat'))  261 us
    dot_general x14, matrix products, product(): jnp.einsum(pattern, left_side, right_side, preferred_element_type=jnp.flo...  31.7 us
    all_to_all x1, waiting for transfers between devices, on_device(): lax.all_to_all(spectra, 'lat', split_axis=2, concat_axis=1, tiled=True)  19.5 us
    all_to_all x1, starting transfers between devices, on_device(): lax.all_to_all(spectra, 'lat', split_axis=2, concat_axis=1, tiled=True)  13.7 us
    all_to_all x1, waiting for transfers between devices, on_device(): lax.all_to_all(back_rows, 'lat', split_axis=2, concat_axis=1, tiled=True)  10.8 us
  transfers between devices with their start and end apart: 5, of which 4 were waited for; matrix products, arithmetic and copies ran while one was open for 9% of the time, Pallas kernels for 0%

commit v1 on v0

--- a/solution.py
+++ b/solution.py
@@ -129,7 +129,9 @@
     spectra = product("bhwc,wkp->bhkpc", normed.astype(jnp.bfloat16), forward_lon).astype(
         jnp.bfloat16
     )
-    column_spectra = lax.all_to_all(spectra, "lat", split_axis=2, concat_axis=1, tiled=True)
+    parts = jnp.split(spectra, lax.axis_size("lat"), axis=2)
+    arrived = lax.all_to_all(jnp.stack(parts), "lat", 0, 0)
+    column_spectra = jnp.concatenate(arrived, axis=1)
     spectra_modes = product("mqhp,bhkpc->bmkqc", latitude, column_spectra).astype(jnp.bfloat16)
     pre_one, hidden, pre_two = spectral_forward(
         spectra_modes, first_form, b_first, second_form, b_second

time: 437 us -> 430 us (0.984)
    all_to_all x1, waiting for transfers between devices: 19.5 us -> 10.2 us  [on_device(): arrived = lax.all_to_all(jnp.stack(parts), 'lat', 0, 0)]
    all_to_all x1, starting transfers between devices: 13.7 us -> 6.14 us  [on_device(): arrived = lax.all_to_all(jnp.stack(parts), 'lat', 0, 0)]
    all_to_all x1, starting transfers between devices: 6.14 us -> 13.7 us  [on_device(): lax.all_to_all(back_rows, 'lat', split_axis=2, concat_axis=1, tiled=True)]
    all_to_all x1, waiting for transfers between devices: 10.8 us -> 17.7 us  [on_device(): lax.all_to_all(back_rows, 'lat', split_axis=2, concat_axis=1, tiled=True)]
where the time goes in v1:
time: 430 us; the launch traced here: 429 us
  waiting for transfers between devices  296 us (69%)
  local copies, waits for them, and re-layouts  38.4 us (9%)
  starting transfers between devices  33.5 us (8%)
  matrix products  33.2 us (8%)
  between operations  14.8 us (3%)
  other arithmetic  13.7 us (3%)
    psum x1, waiting for transfers between devices, on_device(): all_grads = lax.psum(packed, ('dp', 'lat'))  261 us
    dot_general x14, matrix products, product(): jnp.einsum(pattern, left_side, right_side, preferred_element_type=jnp.flo...  33.2 us
    all_to_all x1, waiting for transfers between devices, on_device(): lax.all_to_all(back_rows, 'lat', split_axis=2, concat_axis=1, tiled=True)  17.7 us
    all_to_all x1, starting transfers between devices, on_device(): lax.all_to_all(back_rows, 'lat', split_axis=2, concat_axis=1, tiled=True)  13.7 us
    all_to_all x1, waiting for transfers between devices, on_device(): arrived = lax.all_to_all(jnp.stack(parts), 'lat', 0, 0)  10.2 us
  transfers between devices with their start and end apart: 5, of which 4 were waited for; matrix products, arithmetic and copies ran while one was open for 9% of the time, Pallas kernels for 0%

profile of v1, /device:TPU:1, one launch (start us, length us, event | category | flops | bytes accessed | tf_op | source)
XLA Modules:
  0.0 429.1 jit_solution(5514507537022855947)
XLA Ops:
  8.2 1.7 fusion.41
  9.9 1.8 copy.155
  11.8 13.7 %all-to-all-start.2 = ((bf16[1,3,96,2,768]{4,3,1,0,2:T(2,128)(2,1)}), bf16[1,3,96,2,768]{4,3,1,0,2:T(2,128)(2,1)S(1)}, u32[]{:S(2)}, u32[]{:S(2)}) async-start(bf16[1,3,96,2,768]{4,3,1,0,2:T(2,128)(2,1)} %copy.155), calls=%async_computation.2 | async-start | bytes 1769472 | tf_op jit(solution)/shard_map/all_to_all | solution.py:146
  29.0 1.7 copy.145
  30.7 17.7 %all-to-all-done.2 = bf16[1,3,96,2,768]{4,3,1,0,2:T(2,128)(2,1)S(1)} async-done(((bf16[1,3,96,2,768]{4,3,1,0,2:T(2,128)(2,1)}), bf16[1,3,96,2,768]{4,3,1,0,2:T(2,128)(2,1)S(1)}, u32[]{:S(2)}, u32[]{:S(2)}) %all-to-all-start.2) | async-done | bytes 884768 | tf_op jit(solution)/shard_map/all_to_all | solution.py:146
  48.4 6.1 %all-to-all-start = ((bf16[32,1,3,3,2,768]{5,4,3,2,1,0:T(2,128)(2,1)}), bf16[32,1,3,3,2,768]{5,4,3,2,1,0:T(2,128)(2,1)S(1)}, u32[]{:S(2)}, u32[]{:S(2)}) async-start(bf16[32,1,3,3,2,768]{5,4,3,2,1,0:T(2,128)(2,1)} %copy.145), calls=%async_computation | async-start | bytes 1769472 | tf_op jit(solution)/shard_map/all_to_all | solution.py:133
  62.5 1.4 convert_reduce_fusion.2
  63.9 2.4 reshape.659
  66.3 10.2 %all-to-all-done = bf16[32,1,3,3,2,768]{5,4,3,2,1,0:T(2,128)(2,1)S(1)} async-done(((bf16[32,1,3,3,2,768]{5,4,3,2,1,0:T(2,128)(2,1)}), bf16[32,1,3,3,2,768]{5,4,3,2,1,0:T(2,128)(2,1)S(1)}, u32[]{:S(2)}, u32[]{:S(2)}) %all-to-all-start) | async-done | bytes 884768 | tf_op jit(solution)/shard_map/all_to_all | solution.py:133
  76.5 2.2 fusion.42
  78.7 3.2 reshape.653
  81.9 7.0 %fusion.5 = (f32[96,3,2,8,96]{4,0,1,2,3:T(8,128)S(1)}, f32[8,2,96,96,3,1]{2,3,5,4,1,0:T(8,128)S(1)}) fusion(f32[2,8,96]{2,0,1:T(2,128)S(1)} %copy-done.22, bf16[96,3,2,8,96,1]{4,3,0,2,1,5:T(8,128)(2,1)} %bitcast.491, bf16[8,1,96,2,96]{4,2,1,3,0:T(8,128)(2,1)} %get-tuple-element.18, bf16[8,1,96,2,96]{4,2,1,3,0:T(8,128)(2,1)} %get-tuple-element.17), kind=kOutput, calls=%fused_computation.11 | convolution fusion | flops 198918144 | bytes 5019648 | tf_op jit(solution)/shard_map/bmkqni,nqipo->bmkpno/dot_general | solution.py:65
  90.7 7.2 %convert_reduce_fusion.1 = (f32[2,8,96]{2,0,1:T(2,128)S(1)}, bf16[1,96,3,2,8,96]{5,1,2,3,4,0:T(8,128)(2,1)}, f32[1,96,3,2,8,96]{5,1,2,3,4,0:T(8,128)}, f32[8,2,96,96,3,1]{2,3,5,4,1,0:T(8,128)S(1)}) fusion(f32[2,8,96]{2,0,1:T(2,128)S(1)} %copy-done.22, f32[8,2,96,96,3,1]{2,3,5,4,1,0:T(8,128)S(1)} %get-tuple-element.35, ...), kind=kOutput, calls=%fused_computation.34 | convolution fusion | flops 203340288 | bytes 7680000 | tf_op jit(solution)/shard_map/bmkpno,nqipo->bmkqni/dot_general | solution.py:65
  97.9 1.9 convolution_bitcast_fusion.2
  103.5 3.2 convolution_bitcast_fusion
  106.7 2.0 copy.150
  108.7 2.1 reshape.655
  111.3 1.8 copy.152
  113.8 6.6 %all-to-all-start.1 = ((bf16[1,96,3,2,768]{4,3,2,0,1:T(2,128)(2,1)}), bf16[1,96,3,2,768]{4,3,2,0,1:T(2,128)(2,1)S(1)}, u32[]{:S(2)}, u32[]{:S(2)}) async-start(bf16[1,96,3,2,768]{4,3,2,0,1:T(2,128)(2,1)} %copy.152), calls=%async_computation.1 | async-start | bytes 1769472 | tf_op jit(solution)/shard_map/all_to_all | solution.py:141
  122.9 2.3 maximum_multiply_fusion
  125.3 2.9 fusion.39
  128.2 1.8 copy.163
  130.0 1.9 reshape.695
  131.9 1.6 fusion.45
  133.5 1.8 copy.165
  135.3 6.8 %all-to-all-done.1 = bf16[1,96,3,2,768]{4,3,2,0,1:T(2,128)(2,1)S(1)} async-done(((bf16[1,96,3,2,768]{4,3,2,0,1:T(2,128)(2,1)}), bf16[1,96,3,2,768]{4,3,2,0,1:T(2,128)(2,1)S(1)}, u32[]{:S(2)}, u32[]{:S(2)}) %all-to-all-start.1) | async-done | bytes 884768 | tf_op jit(solution)/shard_map/all_to_all | solution.py:141
  142.1 6.9 %all-to-all-start.3 = ((bf16[1,96,3,2,768]{4,3,2,0,1:T(2,128)(2,1)}), bf16[1,96,3,2,768]{4,3,2,0,1:T(2,128)(2,1)}, u32[]{:S(2)}, u32[]{:S(2)}) async-start(bf16[1,96,3,2,768]{4,3,2,0,1:T(2,128)(2,1)} %copy.165), calls=%async_computation.3 | async-start | bytes 1769472 | tf_op jit(solution)/shard_map/all_to_all | solution.py:154
  149.1 260.8 %all-reduce.2.cloned.1.call-done = f32[297984]{0:T(1024)} async-done(((f32[297984]{0:T(1024)}), f32[297984]{0:T(1024)}) %all-reduce.2.cloned.1.call-update) | async-done | bytes 1191952 | tf_op jit(solution)/shard_map/psum | solution.py:160
  409.9 1.3 fusion.121
  416.1 1.4 fusion.37
  417.5 1.8 copy.166
  420.7 1.6 fusion.33
  (147 shorter events, 27.3 us)
Async XLA Ops:
  8.2 17.2 %copy-start = (bf16[1,3,180,768]{3,2,1,0:T(8,128)(2,1)S(1)}, bf16[1,3,180,768]{3,2,1,0:T(8,128)(2,1)}, u32[]{:S(2)}) copy-start(bf16[1,3,180,768]{3,2,1,0:T(8,128)(2,1)} %param.6) | copy-start | bytes 2488324
  11.8 36.7 %all-to-all-start.2 = ((bf16[1,3,96,2,768]{4,3,1,0,2:T(2,128)(2,1)}), bf16[1,3,96,2,768]{4,3,1,0,2:T(2,128)(2,1)S(1)}, u32[]{:S(2)}, u32[]{:S(2)}) async-start(bf16[1,3,96,2,768]{4,3,1,0,2:T(2,128)(2,1)} %copy.155), calls=%async_computation.2 | async-start | bytes 1769472 | tf_op jit(solution)/shard_map/all_to_all | solution.py:146
  26.1 1.7 copy-start.25
  26.7 1.1 copy-start.23
  28.9 26.7 %copy-start.28 = (f32[2,768]{1,0:T(2,128)S(1)}, f32[2,768]{1,0:T(2,128)}, u32[]{:S(2)}) copy-start(f32[2,768]{1,0:T(2,128)} %param.9) | copy-start | bytes 18436
  48.4 28.1 %all-to-all-start = ((bf16[32,1,3,3,2,768]{5,4,3,2,1,0:T(2,128)(2,1)}), bf16[32,1,3,3,2,768]{5,4,3,2,1,0:T(2,128)(2,1)S(1)}, u32[]{:S(2)}, u32[]{:S(2)}) async-start(bf16[32,1,3,3,2,768]{5,4,3,2,1,0:T(2,128)(2,1)} %copy.145), calls=%async_computation | async-start | bytes 1769472 | tf_op jit(solution)/shard_map/all_to_all | solution.py:133
  56.7 5.9 %copy-start.30 = (f32[3]{0:T(128)}, f32[3]{0:T(128)S(1)}, u32[]{:S(2)}) copy-start(f32[3]{0:T(128)S(1)} %compare_select_fusion) | copy-start | bytes 40
  57.1 5.4 %copy-start.9 = (bf16[96,1,96,2]{2,0,3,1:T(8,128)(2,1)}, bf16[96,1,96,2]{2,0,3,1:T(8,128)(2,1)S(1)}, u32[]{:S(2)}) copy-start(bf16[96,1,96,2]{2,0,3,1:T(8,128)(2,1)S(1)} %get-tuple-element.22) | copy-start | bytes 110596
  58.1 32.4 %copy-start.4 = (bf16[8,1,96,2,96]{2,4,1,3,0:T(8,128)(2,1)}, bf16[8,1,96,2,96]{2,4,1,3,0:T(8,128)(2,1)S(1)}, u32[]{:S(2)}) copy-start(bf16[8,1,96,2,96]{2,4,1,3,0:T(8,128)(2,1)S(1)} %get-tuple-element.19) | copy-start | bytes 884740
  66.3 15.6 %copy-start.22 = (f32[2,8,96]{2,0,1:T(2,128)S(1)}, f32[2,8,96]{2,0,1:T(2,128)}, u32[]{:S(2)}) copy-start(f32[2,8,96]{2,0,1:T(2,128)} %copy.148) | copy-start | bytes 18436
  88.9 9.1 %copy-start.1 = (f32[8,2,96,96,3,1]{2,3,5,4,1,0:T(8,128)}, f32[8,2,96,96,3,1]{2,3,5,4,1,0:T(8,128)S(1)}, u32[]{:S(2)}) copy-start(f32[8,2,96,96,3,1]{2,3,5,4,1,0:T(8,128)S(1)} %get-tuple-element.35) | copy-start | bytes 5308420
  89.7 1.0 copy-start.5
  90.7 7.2 %copy-start.8 = (bf16[96,3,2,8,96]{4,3,0,2,1:T(8,128)(2,1)S(1)}, bf16[96,3,2,8,96]{4,3,0,2,1:T(8,128)(2,1)}, u32[]{:S(2)}) copy-start(bf16[96,3,2,8,96]{4,3,0,2,1:T(8,128)(2,1)} %reshape.653) | copy-start | bytes 2654212
  99.9 2.2 copy-start.7
  108.7 2.1 copy-start.10
  108.7 2.1 copy-start.29
  108.7 2.1 copy-start.31
  111.3 9.2 %copy-start.6 = (f32[1,8,96,96]{3,2,1,0:T(8,128)S(1)}, f32[1,8,96,96]{3,2,1,0:T(8,128)}, u32[]{:S(2)}) copy-start(f32[1,8,96,96]{3,2,1,0:T(8,128)} %fusion.84) | copy-start | bytes 884740
  113.8 9.1 %copy-start.3 = (f32[147456]{0:T(1024)S(1)}, f32[147456]{0:T(1024)}, u32[]{:S(2)}) copy-start(f32[147456]{0:T(1024)} %reshape.666) | copy-start | bytes 1769476
  113.8 28.3 %all-to-all-start.1 = ((bf16[1,96,3,2,768]{4,3,2,0,1:T(2,128)(2,1)}), bf16[1,96,3,2,768]{4,3,2,0,1:T(2,128)(2,1)S(1)}, u32[]{:S(2)}, u32[]{:S(2)}) async-start(bf16[1,96,3,2,768]{4,3,2,0,1:T(2,128)(2,1)} %copy.152), calls=%async_computation.1 | async-start | bytes 1769472 | tf_op jit(solution)/shard_map/all_to_all | solution.py:141
  120.5 289.4 %all-reduce.2.cloned.1.call-start = ((), (), s32[]{:S(2)}) async-start(), calls=%async_computation.4 | async-start | bytes 2383872 | tf_op jit(solution)/shard_map/psum | solution.py:160
  121.6 3.7 copy-start.12
  122.9 2.4 copy-start.13
  128.2 3.7 copy-start.11
  142.1 275.3 %all-to-all-start.3 = ((bf16[1,96,3,2,768]{4,3,2,0,1:T(2,128)(2,1)}), bf16[1,96,3,2,768]{4,3,2,0,1:T(2,128)(2,1)}, u32[]{:S(2)}, u32[]{:S(2)}) async-start(bf16[1,96,3,2,768]{4,3,2,0,1:T(2,128)(2,1)} %copy.165), calls=%async_computation.3 | async-start | bytes 1769472 | tf_op jit(solution)/shard_map/all_to_all | solution.py:154
  411.2 4.8 %copy-start.15 = (bf16[180,96,1]{1,0,2:T(8,128)(2,1)S(1)}, bf16[180,96,1]{1,0,2:T(8,128)(2,1)}, u32[]{:S(2)}) copy-start(bf16[180,96,1]{1,0,2:T(8,128)(2,1)} %copy-done.14) | copy-start | bytes 103684
  411.2 4.8 %copy-start.17 = (bf16[180,96,1]{1,0,2:T(8,128)(2,1)S(1)}, bf16[180,96,1]{1,0,2:T(8,128)(2,1)}, u32[]{:S(2)}) copy-start(bf16[180,96,1]{1,0,2:T(8,128)(2,1)} %copy-done.16) | copy-start | bytes 103684
  411.2 4.8 %copy-start.24 = (f32[3,180]{1,0:T(4,128)S(1)}, f32[3,180]{1,0:T(4,128)}, u32[]{:S(2)}) copy-start(f32[3,180]{1,0:T(4,128)} %copy-done.23) | copy-start | bytes 6484
  416.0 3.2 copy-start.2
  416.1 3.2 copy-start.19
  416.1 3.2 copy-start.21
  416.1 3.2 copy-start.27
  (5 other events, 3.3 us)
Sparse Core Ops, SparseCore 0:
  126.4 283.4 all-reduce.1
